TPU v7x, 256 devices: a whole 4x4x8 slice. The times are simulated.
256 devices in a mesh: dp: 2 (over z_hi), seq: 128 (over y, x, z_lo, core).
Axes of the slice: x: 4, y: 4, z: 8 (z_hi: 2, z_lo: 4; z = z_hi * 4 + z_lo), core: 2. Of those that a mesh axis runs over, the one named last changes fastest.
Arguments:
- signal: bfloat16 [2, 262144, 256], P('dp', 'seq'), may hold values from -6 to 6
- gating: bfloat16 [2, 262144, 256], P('dp', 'seq'), may hold values from -6 to 6
- upstream: bfloat16 [2, 262144, 256], P('dp', 'seq'), may hold values from -1.5 to 1.5
- left_factor: bfloat16 [512, 512, 512], P('seq'), may hold values from -0.25 to 0.25
- right_factor: bfloat16 [512, 512, 512], P('seq'), may hold values from -0.25 to 0.25
Outputs:
- output: bfloat16 [2, 262144, 256], P('dp', 'seq')
- grad_gating: bfloat16 [2, 262144, 256], P('dp', 'seq')
- grad_signal: bfloat16 [2, 262144, 256], P('dp', 'seq')
- grad_left: bfloat16 [512, 512, 512], P('seq')
- grad_right: bfloat16 [512, 512, 512], P('seq')
All inputs are finite; a program needn't handle non-finite values.
Results may differ from a plain program's by a relative error of at most 0.0075.
Values may be sent and summed in bfloat16 or wider, within the bound.
A program may use at most 64 MiB of HBM per device.

v0:
```python
import jax
import jax.numpy as jnp
from jax import lax
from jax.sharding import PartitionSpec as P


def sent_together(arrays, axis, split_dim, concat_dim, along):
    ends, at = ([], 0)
    for a in arrays[:-1]:
        at += a.shape[along]
        ends.append(at)
    both = jnp.concatenate(arrays, axis=along)
    return tuple(
        jnp.split(
            lax.all_to_all(both, axis, split_axis=split_dim, concat_axis=concat_dim, tiled=True),
            ends,
            axis=along,
        )
    )


def over_pieces(x, axis):
    tiles = lax.all_gather(x, axis).astype(jnp.float32)
    return tiles.sum(axis=0)


def column_forward(right_factor, by_column):
    return jnp.einsum(
        "kmi,ikd->mkd", right_factor, by_column, preferred_element_type=jnp.float32
    ).astype(jnp.bfloat16)


def column_backward(right_factor, grad_column):
    return jnp.einsum(
        "kmi,mkd->ikd", right_factor, grad_column, preferred_element_type=jnp.float32
    ).astype(jnp.bfloat16)


def shards(signal, gating, upstream, left_factor, right_factor):
    block_count = left_factor.shape[0]
    block_len = left_factor.shape[1]
    channels = signal.shape[2]
    values = signal.reshape(block_count, block_len, channels)
    gate_rows = gating.reshape(block_count, block_len, channels)
    upstream_rows = upstream.reshape(block_count, block_len, channels)
    mixed_rows = jnp.einsum(
        "ikj,ijd->ikd", left_factor, values, preferred_element_type=jnp.float32
    ).astype(jnp.bfloat16)
    grad_rows = (upstream_rows.astype(jnp.float32) * gate_rows.astype(jnp.float32)).astype(
        jnp.bfloat16
    )
    by_column, grad_column = (
        lax.all_to_all(mixed_rows, "seq", split_axis=1, concat_axis=0, tiled=True),
        lax.all_to_all(grad_rows, "seq", split_axis=1, concat_axis=0, tiled=True),
    )
    second = column_forward(right_factor, by_column)
    grad_second = column_backward(right_factor, grad_column)
    mixed_out, grad_back = sent_together((second, grad_second), "seq", 0, 1, 2)
    mixed_wide = mixed_out.astype(jnp.float32)
    output = (gate_rows.astype(jnp.float32) * mixed_wide).astype(jnp.bfloat16).reshape(signal.shape)
    grad_gate = (
        (upstream_rows.astype(jnp.float32) * mixed_wide).astype(jnp.bfloat16).reshape(signal.shape)
    )
    grad_signal = (
        jnp.einsum("ikj,ikd->ijd", left_factor, grad_back, preferred_element_type=jnp.float32)
        .astype(jnp.bfloat16)
        .reshape(signal.shape)
    )
    left_term = jnp.einsum("ikd,ijd->ikj", grad_back, values, preferred_element_type=jnp.float32)
    right_term = jnp.einsum(
        "mkd,ikd->kmi", grad_column, by_column, preferred_element_type=jnp.float32
    )
    left_sum, right_sum = (
        over_pieces(left_term.astype(jnp.bfloat16), "dp").astype(jnp.float32),
        over_pieces(right_term.astype(jnp.bfloat16), "dp").astype(jnp.float32),
    )
    grad_left = left_sum.astype(jnp.bfloat16)
    grad_right = right_sum.astype(jnp.bfloat16)
    return (output, grad_gate, grad_signal, grad_left, grad_right)


def solution(mesh):
    in_specs = (
        P("dp", "seq", None),
        P("dp", "seq", None),
        P("dp", "seq", None),
        P("seq", None, None),
        P("seq", None, None),
    )
    out_specs = (
        P("dp", "seq", None),
        P("dp", "seq", None),
        P("dp", "seq", None),
        P("seq", None, None),
        P("seq", None, None),
    )
    return jax.shard_map(shards, mesh=mesh, in_specs=in_specs, out_specs=out_specs, check_vma=False)
```

profile of v0, /device:TPU:1, one launch (start us, length us, event | category | flops | bytes accessed | tf_op | source)
XLA Modules:
  0.0 379.8 jit_solution(14072103680214955816)
XLA Ops:
  7.2 2.7 convolution_convert_fusion.5
  9.9 1.8 copy.29
  11.7 14.3 %all-to-all-start = ((bf16[4,512,256]{2,0,1:T(4,128)(2,1)}), bf16[4,512,256]{2,0,1:T(4,128)(2,1)}, u32[]{:S(2)}, u32[]{:S(2)}) async-start(bf16[4,512,256]{2,0,1:T(4,128)(2,1)} %copy.29), calls=%async_computation | async-start | bytes 2097152 | tf_op jit(solution)/shard_map/all_to_all | solution.py:53
  26.0 1.5 fusion.1
  27.5 1.8 copy.32
  29.2 25.8 %all-to-all-done = bf16[4,512,256]{2,0,1:T(4,128)(2,1)} async-done(((bf16[4,512,256]{2,0,1:T(4,128)(2,1)}), bf16[4,512,256]{2,0,1:T(4,128)(2,1)}, u32[]{:S(2)}, u32[]{:S(2)}) %all-to-all-start) | async-done | bytes 1048608 | tf_op jit(solution)/shard_map/all_to_all | solution.py:53
  55.0 7.5 %all-to-all-start.1 = ((bf16[4,512,256]{2,0,1:T(4,128)(2,1)}), bf16[4,512,256]{2,0,1:T(4,128)(2,1)}, u32[]{:S(2)}, u32[]{:S(2)}) async-start(bf16[4,512,256]{2,0,1:T(4,128)(2,1)} %copy.32), calls=%async_computation.1 | async-start | bytes 2097152 | tf_op jit(solution)/shard_map/all_to_all | solution.py:54
  62.5 1.6 copy.30
  64.2 27.5 %all-to-all-done.1 = bf16[4,512,256]{2,0,1:T(4,128)(2,1)} async-done(((bf16[4,512,256]{2,0,1:T(4,128)(2,1)}), bf16[4,512,256]{2,0,1:T(4,128)(2,1)}, u32[]{:S(2)}, u32[]{:S(2)}) %all-to-all-start.1) | async-done | bytes 1048608 | tf_op jit(solution)/shard_map/all_to_all | solution.py:54
  91.7 1.6 copy.33
  93.3 0.8 fusion.3
  94.1 0.1 copy-done.1
  94.3 0.8 fusion.4
  95.0 1.5 pad_maximum_fusion
  96.5 4.5 %copy.35 = bf16[512,4,512]{2,1,0:T(4,128)(2,1)} copy(bf16[512,4,512]{0,2,1:T(8,128)(2,1)} %pad_maximum_fusion) | data formatting | bytes 4194304 | tf_op jit(solution)/shard_map/concatenate | solution.py:12
  101.0 7.5 %all-to-all-start.2 = ((bf16[512,4,512]{2,1,0:T(4,128)(2,1)}), bf16[512,4,512]{2,1,0:T(4,128)(2,1)}, u32[]{:S(2)}, u32[]{:S(2)}) async-start(bf16[512,4,512]{2,1,0:T(4,128)(2,1)} %copy.35), calls=%async_computation.2 | async-start | bytes 4194304 | tf_op jit(solution)/shard_map/all_to_all | solution.py:15
  108.5 0.2 all-gather.7.cloned.1.call-start
  108.8 3.3 convolution_convert_fusion
  112.1 0.0 all-gather.7.cloned.1.call-update
  112.1 0.0 all-gather.5.cloned.1.call-start
  112.1 137.9 %all-to-all-done.2 = bf16[512,4,512]{2,1,0:T(4,128)(2,1)} async-done(((bf16[512,4,512]{2,1,0:T(4,128)(2,1)}), bf16[512,4,512]{2,1,0:T(4,128)(2,1)}, u32[]{:S(2)}, u32[]{:S(2)}) %all-to-all-start.2) | async-done | bytes 2097184 | tf_op jit(solution)/shard_map/all_to_all | solution.py:15
  250.0 2.8 copy.36
  252.8 2.1 fusion.10
  255.0 1.6 copy.45
  256.6 3.4 convolution_convert_fusion.1
  260.0 0.0 all-gather.5.cloned.1.call-update
  260.0 3.3 fusion.5
  263.3 2.3 copy.39
  265.6 3.3 fusion.2
  268.9 5.5 %reduce_sum.25 = bf16[4,512,512]{2,1,0:T(8,128)(2,1)} reduce(bf16[2,4,512,512]{3,2,1,0:T(8,128)(2,1)} %bitcast.45, bf16[]{:T(256)} %constant.3.clone.1), dimensions={0}, to_apply=%region_1.0 | reduce | flops 1048576 | bytes 6291458 | tf_op jit(solution)/shard_map/reduce_sum | solution.py:24
  274.4 93.6 %all-gather.5.cloned.1.call-done = bf16[8,512,512]{2,1,0:T(8,128)(2,1)} async-done(((bf16[4,512,512]{2,1,0:T(8,128)(2,1)}), bf16[8,512,512]{2,1,0:T(8,128)(2,1)}) %all-gather.5.cloned.1.call-update) | async-done | bytes 4194320 | tf_op jit(solution)/shard_map/all_gather | solution.py:23
  368.0 4.9 %reduce_sum.24 = bf16[4,512,512]{2,1,0:T(8,128)(2,1)} reduce(bf16[2,4,512,512]{3,2,1,0:T(8,128)(2,1)} %bitcast.46, bf16[]{:T(256)} %constant.3.clone.1), dimensions={0}, to_apply=%region_0.0 | reduce | flops 1048576 | bytes 6291458 | tf_op jit(solution)/shard_map/reduce_sum | solution.py:24
  (8 shorter events, 0.0 us)
Async XLA Ops:
  7.2 86.2 %copy-start = (bf16[4,512,512]{2,1,0:T(8,128)(2,1)S(1)}, bf16[4,512,512]{2,1,0:T(8,128)(2,1)}, u32[]{:S(2)}) copy-start(bf16[4,512,512]{2,1,0:T(8,128)(2,1)} %param.9) | copy-start | bytes 6291460
  9.9 16.1 %copy-start.2 = (bf16[1,2048,256]{2,1,0:T(8,128)(2,1)S(1)}, bf16[1,2048,256]{2,1,0:T(8,128)(2,1)}, u32[]{:S(2)}) copy-start(bf16[1,2048,256]{2,1,0:T(8,128)(2,1)} %param.7) | copy-start | bytes 3145732
  11.7 43.3 %all-to-all-start = ((bf16[4,512,256]{2,0,1:T(4,128)(2,1)}), bf16[4,512,256]{2,0,1:T(4,128)(2,1)}, u32[]{:S(2)}, u32[]{:S(2)}) async-start(bf16[4,512,256]{2,0,1:T(4,128)(2,1)} %copy.29), calls=%async_computation | async-start | bytes 2097152 | tf_op jit(solution)/shard_map/all_to_all | solution.py:53
  55.0 36.7 %all-to-all-start.1 = ((bf16[4,512,256]{2,0,1:T(4,128)(2,1)}), bf16[4,512,256]{2,0,1:T(4,128)(2,1)}, u32[]{:S(2)}, u32[]{:S(2)}) async-start(bf16[4,512,256]{2,0,1:T(4,128)(2,1)} %copy.32), calls=%async_computation.1 | async-start | bytes 2097152 | tf_op jit(solution)/shard_map/all_to_all | solution.py:54
  93.3 1.0 copy-start.1
  101.0 149.0 %all-to-all-start.2 = ((bf16[512,4,512]{2,1,0:T(4,128)(2,1)}), bf16[512,4,512]{2,1,0:T(4,128)(2,1)}, u32[]{:S(2)}, u32[]{:S(2)}) async-start(bf16[512,4,512]{2,1,0:T(4,128)(2,1)} %copy.35), calls=%async_computation.2 | async-start | bytes 4194304 | tf_op jit(solution)/shard_map/all_to_all | solution.py:15
  108.5 160.4 %all-gather.7.cloned.1.call-start = ((), (), s32[]{:S(2)}) async-start(), calls=%async_computation.4 | async-start | bytes 6291456 | tf_op jit(solution)/shard_map/all_gather | solution.py:23
  112.1 255.9 %all-gather.5.cloned.1.call-start = ((), (), s32[]{:S(2)}) async-start(), calls=%async_computation.3 | async-start | bytes 6291456 | tf_op jit(solution)/shard_map/all_gather | solution.py:23
  263.3 2.4 copy-start.3
Sparse Core Ops, SparseCore 0:
  112.2 124.3 all-gather.6
  260.1 107.8 all-gather.4
where the time goes:
time: 381 us; the launch traced here: 380 us
  waiting for transfers between devices  285 us (75%)
  starting transfers between devices  29.6 us (8%)
  local copies, waits for them, and re-layouts  20.4 us (5%)
  other arithmetic  16.7 us (4%)
  matrix products  14.2 us (4%)
  between operations  14.2 us (4%)
    all_to_all x1, waiting for transfers between devices, sent_together(): lax.all_to_all(both, axis, split_axis=split_dim, concat_axis=concat_dim,...  138 us
    all_gather x2, waiting for transfers between devices, over_pieces(): tiles = lax.all_gather(x, axis).astype(jnp.float32)  93.6 us
    all_to_all x1, waiting for transfers between devices, shards(): lax.all_to_all(grad_rows, 'seq', split_axis=1, concat_axis=0, tiled=True)  27.5 us
    all_to_all x1, waiting for transfers between devices, shards(): lax.all_to_all(mixed_rows, 'seq', split_axis=1, concat_axis=0, tiled=True)  25.8 us
    all_to_all x1, starting transfers between devices, shards(): lax.all_to_all(mixed_rows, 'seq', split_axis=1, concat_axis=0, tiled=True)  14.3 us
    reduce_sum x2, other arithmetic, over_pieces(): return tiles.sum(axis=0)  10.4 us
  transfers between devices with their start and end apart: 5, of which 4 were waited for; matrix products, arithmetic and copies ran while one was open for 9% of the time, Pallas kernels for 0%

commit v1 on v0

--- a/solution.py
+++ b/solution.py
@@ -51,7 +51,12 @@
     )
     by_column, grad_column = (
         lax.all_to_all(mixed_rows, "seq", split_axis=1, concat_axis=0, tiled=True),
-        lax.all_to_all(grad_rows, "seq", split_axis=1, concat_axis=0, tiled=True),
+        jnp.concatenate(
+            lax.all_to_all(
+                jnp.stack(jnp.split(grad_rows, lax.axis_size("seq"), axis=1)), "seq", 0, 0
+            ),
+            axis=0,
+        ),
     )
     second = column_forward(right_factor, by_column)
     grad_second = column_backward(right_factor, grad_column)

time: 381 us -> 379 us (level)
  no operation moved by 1% of the time
where the time goes in v1:
time: 379 us; the launch traced here: 378 us
  waiting for transfers between devices  283 us (75%)
  starting transfers between devices  28.7 us (8%)
  local copies, waits for them, and re-layouts  21 us (6%)
  other arithmetic  16.7 us (4%)
  between operations  14.7 us (4%)
  matrix products  14.2 us (4%)
    all_to_all x1, waiting for transfers between devices, sent_together(): lax.all_to_all(both, axis, split_axis=split_dim, concat_axis=concat_dim,...  138 us
    all_gather x2, waiting for transfers between devices, over_pieces(): tiles = lax.all_gather(x, axis).astype(jnp.float32)  93.6 us
    all_to_all x1, waiting for transfers between devices, shards(): lax.all_to_all(jnp.stack(jnp.split(grad_rows, lax.axis_size('seq'), axis=...  26.8 us
    all_to_all x1, waiting for transfers between devices, shards(): lax.all_to_all(mixed_rows, 'seq', split_axis=1, concat_axis=0, tiled=True)  24.3 us
    all_to_all x1, starting transfers between devices, shards(): lax.all_to_all(mixed_rows, 'seq', split_axis=1, concat_axis=0, tiled=True)  14.3 us
    reduce_sum x2, other arithmetic, over_pieces(): return tiles.sum(axis=0)  10.4 us
  transfers between devices with their start and end apart: 5, of which 4 were waited for; matrix products, arithmetic and copies ran while one was open for 9% of the time, Pallas kernels for 0%

profile of v1, /device:TPU:1, one launch (start us, length us, event | category | flops | bytes accessed | tf_op | source)
XLA Modules:
  0.0 377.9 jit_solution(4375716928952038583)
XLA Ops:
  7.2 0.0 copy-start
  7.2 2.7 convolution_convert_fusion.5
  9.9 1.8 copy.27
  11.7 14.3 %all-to-all-start = ((bf16[4,512,256]{2,0,1:T(4,128)(2,1)}), bf16[4,512,256]{2,0,1:T(4,128)(2,1)}, u32[]{:S(2)}, u32[]{:S(2)}) async-start(bf16[4,512,256]{2,0,1:T(4,128)(2,1)} %copy.27), calls=%async_computation | async-start | bytes 2097152 | tf_op jit(solution)/shard_map/all_to_all | solution.py:53
  26.0 1.5 fusion.1
  29.8 1.0 copy-done.4
  30.8 24.3 %all-to-all-done = bf16[4,512,256]{2,0,1:T(4,128)(2,1)} async-done(((bf16[4,512,256]{2,0,1:T(4,128)(2,1)}), bf16[4,512,256]{2,0,1:T(4,128)(2,1)}, u32[]{:S(2)}, u32[]{:S(2)}) %all-to-all-start) | async-done | bytes 1048608 | tf_op jit(solution)/shard_map/all_to_all | solution.py:53
  55.0 6.7 %all-to-all-start.1 = ((bf16[128,4,4,256]{3,2,1,0:T(4,128)(2,1)}), bf16[128,4,4,256]{3,2,1,0:T(4,128)(2,1)S(1)}, u32[]{:S(2)}, u32[]{:S(2)}) async-start(bf16[128,4,4,256]{3,2,1,0:T(4,128)(2,1)} %copy-done.4), calls=%async_computation.1 | async-start | bytes 2097152 | tf_op jit(solution)/shard_map/all_to_all | solution.py:55
  61.7 2.6 copy.28
  64.3 26.8 %all-to-all-done.1 = bf16[128,4,4,256]{3,2,1,0:T(4,128)(2,1)S(1)} async-done(((bf16[128,4,4,256]{3,2,1,0:T(4,128)(2,1)}), bf16[128,4,4,256]{3,2,1,0:T(4,128)(2,1)S(1)}, u32[]{:S(2)}, u32[]{:S(2)}) %all-to-all-start.1) | async-done | bytes 1048608 | tf_op jit(solution)/shard_map/all_to_all | solution.py:55
  91.1 0.8 fusion.4
  91.8 0.5 copy-done.1
  92.3 0.8 fusion.3
  93.1 1.5 pad_maximum_fusion
  94.6 4.5 %copy.31 = bf16[512,4,512]{2,1,0:T(4,128)(2,1)} copy(bf16[512,4,512]{0,2,1:T(8,128)(2,1)} %pad_maximum_fusion) | data formatting | bytes 4194304 | tf_op jit(solution)/shard_map/concatenate | solution.py:12
  99.1 7.5 %all-to-all-start.2 = ((bf16[512,4,512]{2,1,0:T(4,128)(2,1)}), bf16[512,4,512]{2,1,0:T(4,128)(2,1)}, u32[]{:S(2)}, u32[]{:S(2)}) async-start(bf16[512,4,512]{2,1,0:T(4,128)(2,1)} %copy.31), calls=%async_computation.2 | async-start | bytes 4194304 | tf_op jit(solution)/shard_map/all_to_all | solution.py:15
  106.6 0.2 all-gather.7.cloned.1.call-start
  106.8 3.3 convolution_convert_fusion
  110.1 0.0 all-gather.7.cloned.1.call-update
  110.2 0.0 all-gather.5.cloned.1.call-start
  110.2 137.9 %all-to-all-done.2 = bf16[512,4,512]{2,1,0:T(4,128)(2,1)} async-done(((bf16[512,4,512]{2,1,0:T(4,128)(2,1)}), bf16[512,4,512]{2,1,0:T(4,128)(2,1)}, u32[]{:S(2)}, u32[]{:S(2)}) %all-to-all-start.2) | async-done | bytes 2097184 | tf_op jit(solution)/shard_map/all_to_all | solution.py:15
  248.1 2.8 copy.32
  250.9 2.1 fusion.10
  253.1 1.6 copy.41
  254.7 3.4 convolution_convert_fusion.1
  258.0 0.0 all-gather.5.cloned.1.call-update
  258.1 3.3 fusion.5
  261.3 2.3 copy.35
  263.7 3.3 fusion.2
  267.0 5.5 %reduce_sum.25 = bf16[4,512,512]{2,1,0:T(8,128)(2,1)} reduce(bf16[2,4,512,512]{3,2,1,0:T(8,128)(2,1)} %bitcast.554, bf16[]{:T(256)} %constant.3.clone.1), dimensions={0}, to_apply=%region_1.0 | reduce | flops 1048576 | bytes 6291458 | tf_op jit(solution)/shard_map/reduce_sum | solution.py:24
  272.5 93.6 %all-gather.5.cloned.1.call-done = bf16[8,512,512]{2,1,0:T(8,128)(2,1)} async-done(((bf16[4,512,512]{2,1,0:T(8,128)(2,1)}), bf16[8,512,512]{2,1,0:T(8,128)(2,1)}) %all-gather.5.cloned.1.call-update) | async-done | bytes 4194320 | tf_op jit(solution)/shard_map/all_gather | solution.py:23
  366.1 4.9 %reduce_sum.24 = bf16[4,512,512]{2,1,0:T(8,128)(2,1)} reduce(bf16[2,4,512,512]{3,2,1,0:T(8,128)(2,1)} %bitcast.555, bf16[]{:T(256)} %constant.3.clone.1), dimensions={0}, to_apply=%region_0.0 | reduce | flops 1048576 | bytes 6291458 | tf_op jit(solution)/shard_map/reduce_sum | solution.py:24
  (136 shorter events, 1.8 us)
Async XLA Ops:
  7.2 83.9 %copy-start = (bf16[4,512,512]{2,1,0:T(8,128)(2,1)S(1)}, bf16[4,512,512]{2,1,0:T(8,128)(2,1)}, u32[]{:S(2)}) copy-start(bf16[4,512,512]{2,1,0:T(8,128)(2,1)} %param.9) | copy-start | bytes 6291460
  9.9 16.1 %copy-start.2 = (bf16[1,2048,256]{2,1,0:T(8,128)(2,1)S(1)}, bf16[1,2048,256]{2,1,0:T(8,128)(2,1)}, u32[]{:S(2)}) copy-start(bf16[1,2048,256]{2,1,0:T(8,128)(2,1)} %param.7) | copy-start | bytes 3145732
  11.7 43.3 %all-to-all-start = ((bf16[4,512,256]{2,0,1:T(4,128)(2,1)}), bf16[4,512,256]{2,0,1:T(4,128)(2,1)}, u32[]{:S(2)}, u32[]{:S(2)}) async-start(bf16[4,512,256]{2,0,1:T(4,128)(2,1)} %copy.27), calls=%async_computation | async-start | bytes 2097152 | tf_op jit(solution)/shard_map/all_to_all | solution.py:53
  29.8 1.0 copy-start.4
  55.0 36.1 %all-to-all-start.1 = ((bf16[128,4,4,256]{3,2,1,0:T(4,128)(2,1)}), bf16[128,4,4,256]{3,2,1,0:T(4,128)(2,1)S(1)}, u32[]{:S(2)}, u32[]{:S(2)}) async-start(bf16[128,4,4,256]{3,2,1,0:T(4,128)(2,1)} %copy-done.4), calls=%async_computation.1 | async-start | bytes 2097152 | tf_op jit(solution)/shard_map/all_to_all | solution.py:55
  91.1 1.2 copy-start.1
  99.1 149.0 %all-to-all-start.2 = ((bf16[512,4,512]{2,1,0:T(4,128)(2,1)}), bf16[512,4,512]{2,1,0:T(4,128)(2,1)}, u32[]{:S(2)}, u32[]{:S(2)}) async-start(bf16[512,4,512]{2,1,0:T(4,128)(2,1)} %copy.31), calls=%async_computation.2 | async-start | bytes 4194304 | tf_op jit(solution)/shard_map/all_to_all | solution.py:15
  106.6 160.4 %all-gather.7.cloned.1.call-start = ((), (), s32[]{:S(2)}) async-start(), calls=%async_computation.4 | async-start | bytes 6291456 | tf_op jit(solution)/shard_map/all_gather | solution.py:23
  110.2 255.9 %all-gather.5.cloned.1.call-start = ((), (), s32[]{:S(2)}) async-start(), calls=%async_computation.3 | async-start | bytes 6291456 | tf_op jit(solution)/shard_map/all_gather | solution.py:23
  261.3 2.4 copy-start.3
Sparse Core Ops, SparseCore 0:
  110.3 124.3 all-gather.6
  258.2 107.8 all-gather.4
